TPU v7x, 512 devices: a whole 4x8x8 slice. The times are simulated.
512 devices in a mesh: seq: 64 (over z, x, core), mlp: 8 (over y).
Axes of the slice: x: 4, y: 8, z: 8, core: 2. Of those that a mesh axis runs over, the one named last changes fastest.
Arguments:
- tokens: bfloat16 [4, 48, 2048], P(None, None, 'seq'), may hold values from -20 to 20
- lengths: int32 [48], replicated, may hold values from 1 to 8192, 48960 in all
- slopes: float32 [16], P('mlp'), may hold values from 1.5258789e-05 to 0.0625
- ln1_gain: float32 [2048], P('seq'), may hold values from 0.1 to 1.9
- ln1_bias: float32 [2048], P('seq'), may hold values from -3 to 3
- w_qkv: bfloat16 [2048, 6144], P('seq', 'mlp'), may hold values from -0.125 to 0.125
- b_qkv: float32 [6144], P('mlp'), may hold values from -3 to 3
- keys: bfloat16 [65536, 2048], P('seq', 'mlp'), may hold values from -200 to 200
- values: bfloat16 [65536, 2048], P('seq', 'mlp'), may hold values from -5 to 5
- w_dense: bfloat16 [2048, 2048], P('mlp', 'seq'), may hold values from -0.125 to 0.125
- b_dense: float32 [2048], P('seq'), may hold values from -2 to 2
- ln2_gain: float32 [2048], P('seq'), may hold values from 0.1 to 1.9
- ln2_bias: float32 [2048], P('seq'), may hold values from -3 to 3
- w_up: bfloat16 [2048, 8192], P('seq', 'mlp'), may hold values from -0.125 to 0.125
- b_up: float32 [8192], P('mlp'), may hold values from -3 to 3
- w_down: bfloat16 [8192, 2048], P('mlp', 'seq'), may hold values from -0.0625 to 0.0625
- b_down: float32 [2048], P('seq'), may hold values from -2 to 2
Outputs:
- attended: bfloat16 [4, 48, 2048], P(None, None, 'seq')
- mixed: bfloat16 [4, 48, 2048], P(None, None, 'seq')
Inputs may be any that keep to these rules, and one draw needn't show every extreme that they name: `lengths`: slots after the last request's 4 drafted slots hold no request's data.
All inputs are finite; a program needn't handle non-finite values.
Results may differ from a plain program's by a relative error of at most 0.008.
The roundings to bfloat16 on the way count: a program that leaves them out, or rounds other values in their place, can miss the bound.
Values may be sent and summed in bfloat16 or wider, within the bound.
A program may use at most 64 MiB of HBM per device.

v0:
```python
import math

import jax
import jax.numpy as jnp
from jax import lax
from jax.sharding import PartitionSpec as P

D = 2048
HD = 128
STEPS = 4


NEG = -1e30
EPS = 1e-05


def gelu_tanh(value):
    return (
        0.5
        * value
        * (1.0 + jnp.tanh(0.7978845608028654 * (value + 0.044715 * value * value * value)))
    )


def normalize_rows(rows, total, total_sq, gain, shift):
    mean = total / D
    spread = total_sq / D - mean * mean
    return ((rows - mean[..., None]) * lax.rsqrt(spread + EPS)[..., None] * gain + shift).astype(
        jnp.bfloat16
    )


def local(
    tokens,
    lengths,
    slopes,
    ln1_gain,
    ln1_bias,
    w_qkv,
    b_qkv,
    keys,
    values,
    w_dense,
    b_dense,
    ln2_gain,
    ln2_bias,
    w_up,
    b_up,
    w_down,
    b_down,
):
    requests = lengths.shape[0]
    spans = lengths + STEPS
    starts = jnp.cumsum(spans) - spans
    ends = starts + spans
    slot_count = keys.shape[0]
    width_local = keys.shape[1]
    heads_local = slopes.shape[0]
    block = min(512, slot_count)
    seq_place = lax.axis_index("seq")
    base = seq_place * slot_count
    request_ids = jnp.arange(requests, dtype=jnp.int32)
    layer_keys = keys
    layer_values = values
    count = tokens.shape[0]
    inputs = tokens.astype(jnp.float32)
    total, total_sq = lax.psum((jnp.sum(inputs, axis=-1), jnp.sum(inputs * inputs, axis=-1)), "seq")
    normed = normalize_rows(inputs, total, total_sq, ln1_gain, ln1_bias)
    flat = normed.reshape(count * requests, -1)
    partial_qkv = jnp.dot(flat, w_qkv, preferred_element_type=jnp.float32)
    rounded = (lax.psum(partial_qkv, "seq") + b_qkv).astype(jnp.bfloat16)
    rounded = rounded.reshape(count, requests, heads_local, 3, HD)
    queries = rounded[:, :, :, 0, :].reshape(count, requests, width_local)
    new_keys = rounded[:, :, :, 1, :].reshape(count * requests, width_local)
    new_values = rounded[:, :, :, 2, :].reshape(count * requests, width_local)
    local_slot = (
        (starts + lengths)[None, :] + (0 + jnp.arange(count, dtype=jnp.int32))[:, None] - base
    )
    inside = (local_slot >= 0) & (local_slot < slot_count)
    target = jnp.where(inside, local_slot, slot_count).reshape(-1)
    layer_keys = layer_keys.at[target].set(new_keys, mode="drop")
    layer_values = layer_values.at[target].set(new_values, mode="drop")

    def visit(index, carry):
        maxima, totals, weighted = carry
        offset_slot = index * block
        key_rows = lax.dynamic_slice_in_dim(layer_keys, offset_slot, block, 0)
        value_rows = lax.dynamic_slice_in_dim(layer_values, offset_slot, block, 0).reshape(
            block, heads_local, HD
        )
        positions = base + offset_slot + jnp.arange(block, dtype=jnp.int32)
        member = (positions[:, None] >= starts[None, :]) & (positions[:, None] < ends[None, :])
        member_half = member.astype(jnp.bfloat16)
        member_full = member.astype(jnp.float32)
        offset = positions - jnp.sum(jnp.where(member, starts[None, :], 0), axis=1)
        length_of = jnp.sum(jnp.where(member, lengths[None, :], 0), axis=1)
        owner = jnp.sum(jnp.where(member, request_ids[None, :], 0), axis=1)
        present = jnp.any(member, axis=1)
        next_max, next_tot, next_wt = ([], [], [])
        for item in range(count):
            reach = length_of + 0 + item
            valid = present & (offset <= reach)
            picked = jnp.dot(member_half, queries[item], preferred_element_type=jnp.float32)
            scores = jnp.sum(
                (picked * key_rows).reshape(block, heads_local, HD), axis=-1
            ) / math.sqrt(HD)
            scores = scores - slopes[None, :] * (reach - offset).astype(jnp.float32)[:, None]
            scores = jnp.where(valid[:, None], scores, NEG)
            usable = member & valid[:, None]
            block_max = jnp.max(jnp.where(usable[:, :, None], scores[:, None, :], NEG), axis=0)
            fresh = jnp.maximum(maxima[item], block_max)
            weights = jnp.where(
                valid[:, None], jnp.exp(scores - jnp.take(fresh, owner, axis=0)), 0.0
            )
            decay = jnp.exp(maxima[item] - fresh)
            block_tot = jnp.einsum(
                "jr,jh->rh", member_full, weights, precision=lax.Precision.HIGHEST
            )
            product = (weights[:, :, None] * value_rows).reshape(block, width_local)
            block_wt = jnp.einsum(
                "jr,jc->rc", member_full, product, precision=lax.Precision.HIGHEST
            )
            next_max.append(fresh)
            next_tot.append(totals[item] * decay + block_tot)
            next_wt.append(weighted[item] * jnp.repeat(decay, HD, axis=-1) + block_wt)
        return (jnp.stack(next_max), jnp.stack(next_tot), jnp.stack(next_wt))

    start = (
        jnp.full((count, requests, heads_local), NEG, jnp.float32),
        jnp.zeros((count, requests, heads_local), jnp.float32),
        jnp.zeros((count, requests, width_local), jnp.float32),
    )
    maxima, totals, weighted = lax.fori_loop(0, slot_count // block, visit, start)
    top = lax.pmax(maxima, "seq")
    decay = jnp.exp(maxima - top)
    totals, weighted = lax.psum((totals * decay, weighted * jnp.repeat(decay, HD, axis=-1)), "seq")
    attention = (weighted / jnp.repeat(totals, HD, axis=-1)).astype(jnp.bfloat16)
    dense = (
        lax.psum(
            jnp.dot(
                attention.reshape(count * requests, width_local),
                w_dense,
                preferred_element_type=jnp.float32,
            ),
            "mlp",
        )
        + b_dense
    )
    attended = dense.astype(jnp.bfloat16).reshape(count, requests, -1)
    hidden = (inputs.reshape(count * requests, -1) + dense).astype(jnp.bfloat16)
    hidden_full = hidden.astype(jnp.float32)
    second, second_sq = lax.psum(
        (jnp.sum(hidden_full, axis=-1), jnp.sum(hidden_full * hidden_full, axis=-1)), "seq"
    )
    normed_second = normalize_rows(hidden_full, second, second_sq, ln2_gain, ln2_bias)
    partial_value = jnp.dot(normed_second, w_up, preferred_element_type=jnp.float32)
    activated = gelu_tanh(lax.psum(partial_value, "seq") + b_up).astype(jnp.bfloat16)
    downward = (
        lax.psum(jnp.dot(activated, w_down, preferred_element_type=jnp.float32), "mlp") + b_down
    )
    mixed = (hidden_full + downward).astype(jnp.bfloat16).reshape(count, requests, -1)
    attended, mixed, keys, values = (attended, mixed, layer_keys, layer_values)
    return (attended, mixed)


def solution(mesh):
    in_specs = (
        P(None, None, "seq"),
        P(),
        P("mlp"),
        P("seq"),
        P("seq"),
        P("seq", "mlp"),
        P("mlp"),
        P("seq", "mlp"),
        P("seq", "mlp"),
        P("mlp", "seq"),
        P("seq"),
        P("seq"),
        P("seq"),
        P("seq", "mlp"),
        P("mlp"),
        P("mlp", "seq"),
        P("seq"),
    )
    out_specs = (P(None, None, "seq"), P(None, None, "seq"))
    return jax.shard_map(local, mesh=mesh, in_specs=in_specs, out_specs=out_specs, check_vma=False)
```

profile of v0, /device:TPU:1, one launch (start us, length us, event | category | flops | bytes accessed | tf_op | source)
XLA Modules:
  0.0 1061.2 jit_solution(10129479071584878941)
XLA Ops:
  7.2 0.7 copy-done.3
  8.0 131.2 %all-reduce.1 = (f32[4,48]{1,0:T(4,128)S(1)}, f32[4,48]{1,0:T(4,128)S(1)}) all-reduce(f32[4,48]{1,0:T(4,128)S(1)} %get-tuple-element.325, f32[4,48]{1,0:T(4,128)S(1)} %get-tuple-element.324), channel_id=1, replica_groups=mesh['seq'=64,'mlp'=8] {'seq'}, use_global_device_ids=true, to_apply=%region_4.5 | all-reduce | flops 384 | bytes 3072 | tf_op jit(solution)/shard_map/psum | solution.py:67
  139.2 0.6 copy-done.9
  140.1 0.7 copy-done.4
  140.8 1.1 fusion.88
  141.9 0.6 copy-done.5
  143.0 189.5 %all-reduce.6.cloned.1.call-done = f32[192,768]{1,0:T(8,128)} async-done(((f32[192,768]{1,0:T(8,128)}), f32[192,768]{1,0:T(8,128)}) %all-reduce.6.cloned.1.call-update) | async-done | bytes 589840 | tf_op jit(solution)/shard_map/psum | solution.py:71
  332.5 1.1 add_convert_fusion
  333.7 1.9 slice_reduce_fusion
  335.7 1.6 scatter_custom_fusion
  337.3 1.6 scatter_custom_fusion.1
  338.9 0.6 copy-done.7
  339.6 27.5 %while.18 = (s32[]{:T(128)}, f32[4,48,2]{1,2,0:T(2,128)S(1)}, f32[4,48,2]{1,2,0:T(2,128)S(1)}, f32[4,48,256]{2,1,0:T(8,128)S(1)}, s32[]{:T(128)}, /*index=5*/s32...) while((s32[]{:T(128)}, f32[4,48,2]{1,2,0:T(2,128)S(1)}, ...), condition=%wide.region_21.23_spmd.clone, body=%wide.region_8.22_spmd.clone.sunk | while | flops 359363328 | bytes 9196599 | solution.py:133
  342.0 1.0 gather_fusion.1
  343.2 1.0 gather_fusion.2
  344.5 1.0 gather_fusion.3
  345.7 1.0 gather_fusion
  347.1 0.6 mul.639
  347.9 0.4 fusion.137
  348.4 0.6 mul.640
  349.3 0.4 fusion.138
  349.8 0.6 mul.641
  350.6 0.4 fusion.139
  351.1 0.6 mul.638
  351.9 0.4 fusion.136
  355.8 1.0 gather_fusion.1
  357.0 1.0 gather_fusion.2
  358.3 1.0 gather_fusion.3
  359.5 1.0 gather_fusion
  360.9 0.6 mul.639
  361.7 0.4 fusion.137
  362.2 0.6 mul.640
  363.6 0.6 mul.641
  364.9 0.6 mul.638
  367.1 125.8 %pmax.7 = f32[4,48,2]{1,2,0:T(2,128)S(1)} all-reduce(f32[4,48,2]{1,2,0:T(2,128)S(1)} %get-tuple-element.220), channel_id=1, replica_groups=mesh['seq'=64,'mlp'=8] {'seq'}, use_global_device_ids=true, to_apply=%region_22.24 | all-reduce | flops 384 | bytes 3072 | tf_op jit(solution)/shard_map/pmax | solution.py:134
  493.5 0.7 mul.396
  494.4 127.4 %psum.74 = f32[4,48,2]{1,2,0:T(2,128)S(1)} all-reduce(f32[4,48,2]{1,2,0:T(2,128)S(1)} %bitcast.286), channel_id=1, replica_groups=mesh['seq'=64,'mlp'=8] {'seq'}, use_global_device_ids=true, to_apply=%region_24.26 | all-reduce | flops 384 | bytes 3072 | tf_op jit(solution)/shard_map/psum | solution.py:136
  622.4 60.2 %all-reduce.8.cloned.1.call-done = f32[4,48,256]{2,1,0:T(8,128)} async-done(((f32[4,48,256]{2,1,0:T(8,128)}), f32[4,48,256]{2,1,0:T(8,128)}) %all-reduce.8.cloned.1.call-update) | async-done | bytes 196624 | tf_op jit(solution)/shard_map/psum | solution.py:136
  682.6 1.0 divide_convert_fusion
  683.7 22.7 %psum.75 = f32[192,32]{0,1:T(8,128)S(1)} all-reduce(f32[192,32]{0,1:T(8,128)S(1)} %fusion.89), channel_id=1, replica_groups=mesh['seq'=64,'mlp'=8] {'mlp'}, use_global_device_ids=true, to_apply=%region_25.27 | all-reduce | flops 6144 | bytes 49152 | tf_op jit(solution)/shard_map/psum | solution.py:139
  706.5 132.8 %all-reduce = (f32[192]{0:T(256)S(1)}, f32[192]{0:T(256)S(1)}) all-reduce(f32[192]{0:T(256)S(1)} %get-tuple-element.327, f32[192]{0:T(256)S(1)} %get-tuple-element.326), channel_id=1, replica_groups=mesh['seq'=64,'mlp'=8] {'seq'}, use_global_device_ids=true, to_apply=%region_29.31 | all-reduce | flops 384 | bytes 3072 | tf_op jit(solution)/shard_map/psum | solution.py:152
  839.3 0.6 copy-done.13
  840.0 1.3 fusion.76
  841.4 0.6 copy.180
  842.0 187.8 %all-reduce.10.cloned.1.call-done = f32[192,1024]{1,0:T(8,128)} async-done(((f32[192,1024]{1,0:T(8,128)}), f32[192,1024]{1,0:T(8,128)}) %all-reduce.10.cloned.1.call-update) | async-done | bytes 786448 | tf_op jit(solution)/shard_map/psum | solution.py:157
  1029.8 1.5 fusion.62
  1031.3 22.6 %psum.79 = f32[192,32]{0,1:T(8,128)S(1)} all-reduce(f32[192,32]{0,1:T(8,128)S(1)} %fusion.62), channel_id=1, replica_groups=mesh['seq'=64,'mlp'=8] {'mlp'}, use_global_device_ids=true, to_apply=%region_31.33 | all-reduce | flops 6144 | bytes 49152 | tf_op jit(solution)/shard_map/psum | solution.py:159
  1054.0 0.6 copy.181
  (166 shorter events, 14.8 us)
Async XLA Ops:
  7.2 832.1 %copy-start = (bf16[32,1024]{1,0:T(8,128)(2,1)S(1)}, bf16[32,1024]{1,0:T(8,128)(2,1)}, u32[]{:S(2)}) copy-start(bf16[32,1024]{1,0:T(8,128)(2,1)} %param.34) | copy-start | bytes 196612
  7.2 325.3 %all-reduce.6.cloned.1.call-start = ((), (), s32[]{:S(2)}) async-start(), calls=%async_computation | async-start | bytes 1179648 | tf_op jit(solution)/shard_map/psum | solution.py:71
  7.2 0.8 copy-start.3
  139.2 0.7 copy-start.9
  139.2 0.7 copy-start.10
  140.0 0.8 copy-start.4
  141.9 0.7 copy-start.5
  141.9 540.7 %all-reduce.8.cloned.1.call-start = ((), (), s32[]{:S(2)}) async-start(), calls=%async_computation.1 | async-start | bytes 393216 | tf_op jit(solution)/shard_map/psum | solution.py:136
  142.8 189.6 %copy-start.8 = (f32[768]{0:T(1024)S(1)}, f32[768]{0:T(1024)}, u32[]{:S(2)}) copy-start(f32[768]{0:T(1024)} %param.27) | copy-start | bytes 9220
  333.7 2.0 copy-start.2
  335.6 1.7 copy-start.1
  338.9 0.7 copy-start.7
  494.2 535.5 %all-reduce.10.cloned.1.call-start = ((), (), s32[]{:S(2)}) async-start(), calls=%async_computation.2 | async-start | bytes 1572864 | tf_op jit(solution)/shard_map/psum | solution.py:157
  622.3 61.2 %copy-start.6 = (bf16[256,32]{0,1:T(8,128)(2,1)S(1)}, bf16[256,32]{0,1:T(8,128)(2,1)}, u32[]{:S(2)}) copy-start(bf16[256,32]{0,1:T(8,128)(2,1)} %param.30) | copy-start | bytes 49156
  683.7 22.7 %copy-start.11 = (f32[32]{0:T(128)S(1)}, f32[32]{0:T(128)}, u32[]{:S(2)}) copy-start(f32[32]{0:T(128)} %param.31) | copy-start | bytes 388
  839.3 0.7 copy-start.13
  839.3 0.7 copy-start.14
  841.3 188.5 %copy-start.15 = (bf16[1024,32]{0,1:T(8,128)(2,1)S(1)}, bf16[1024,32]{0,1:T(8,128)(2,1)}, u32[]{:S(2)}) copy-start(bf16[1024,32]{0,1:T(8,128)(2,1)} %param.36) | copy-start | bytes 196612
  841.4 188.4 %copy-start.16 = (f32[1024]{0:T(1024)S(1)}, f32[1024]{0:T(1024)}, u32[]{:S(2)}) copy-start(f32[1024]{0:T(1024)} %param.35) | copy-start | bytes 12292
  1031.3 22.6 %copy-start.12 = (f32[32]{0:T(128)S(1)}, f32[32]{0:T(128)}, u32[]{:S(2)}) copy-start(f32[32]{0:T(128)} %param.37) | copy-start | bytes 388
Sparse Core Ops, SparseCore 0:
  142.0 190.4 all-reduce.5
  494.3 188.2 all-reduce.7
  841.4 188.3 all-reduce.9
where the time goes:
time: 1070 us; the launch traced here: 1060 us
  blocking collectives  562 us (53%)
  waiting for transfers between devices  438 us (41%)
  local copies, waits for them, and re-layouts  30 us (3%)
  between operations  14.1 us (1%)
  matrix products  11.2 us (1%)
    psum x1, waiting for transfers between devices, local(): rounded = (lax.psum(partial_qkv, 'seq') + b_qkv).astype(jnp.bfloat16)  190 us
    psum x1, waiting for transfers between devices, local(): lax.psum(partial_value, 'seq') + b_up  188 us
    psum x1, blocking collectives, local(): lax.psum((jnp.sum(hidden_full, axis=-1), jnp.sum(hidden_full * hidden_ful...  133 us
    psum x1, blocking collectives, local(): lax.psum((jnp.sum(inputs, axis=-1), jnp.sum(inputs * inputs, axis=-1)), '...  131 us
    psum x1, blocking collectives, local(): lax.psum((totals * decay, weighted * jnp.repeat(decay, HD, axis=-1)), 'seq')  127 us
    pmax x1, blocking collectives, local(): top = lax.pmax(maxima, 'seq')  126 us
    psum x1, waiting for transfers between devices, local(): lax.psum((totals * decay, weighted * jnp.repeat(decay, HD, axis=-1)), 'seq')  60.2 us
    psum x1, blocking collectives, local(): lax.psum(jnp.dot(attention.reshape(count * requests, width_local), w_dens...  22.7 us
  transfers between devices with their start and end apart: 3, of which 3 were waited for; matrix products, arithmetic and copies ran while one was open for 0% of the time, Pallas kernels for 0%

commit v1 on v0

v1 whole, which is shorter than its diff:
```python
import math

import jax
import jax.numpy as jnp
from jax import lax
from jax.experimental import pallas as pl
from jax.experimental.pallas import tpu as pltpu
from jax.sharding import PartitionSpec as P

HD = 128
STEPS = 4
GROUP = 8
ROWS = 24
LANES = 128
NEG = -1e30
FLOOR = -1e29
EPS = 1e-05
MESH = pl.DeviceIdType.MESH

F32 = jnp.float32
BF16 = jnp.bfloat16
NT = (((1,), (1,)), ((), ()))


def gelu_tanh(value):
    return (
        0.5
        * value
        * (1.0 + jnp.tanh(0.7978845608028654 * (value + 0.044715 * value * value * value)))
    )


def dot(a, b):
    return jnp.dot(a, b, preferred_element_type=F32)


def dot_nt(a, b):
    return lax.dot_general(a, b, NT, preferred_element_type=F32)


def iota(shape, dim):
    return lax.broadcasted_iota(jnp.int32, shape, dim)


def to_row(columns):
    lane, row = iota((ROWS, LANES), 1), iota((ROWS, LANES), 0)
    packed = jnp.zeros((ROWS, LANES), F32)
    for i, column in enumerate(columns):
        packed = jnp.where(lane == row + 32 * i, column, packed)
    return jnp.sum(packed, axis=0, keepdims=True)


def to_column(row, i):
    lane, place = iota((ROWS, LANES), 1), iota((ROWS, LANES), 0)
    return jnp.sum(jnp.where(lane == place + 32 * i, row, 0.0), axis=1, keepdims=True)


def kernel(
    features,
    tokens,
    lengths,
    slopes,
    ln1_gain,
    ln1_bias,
    w_qkv,
    b_qkv,
    keys,
    values,
    w_dense,
    b_dense,
    ln2_gain,
    ln2_bias,
    w_up,
    b_up,
    w_down,
    b_down,
    attended_out,
    mixed_out,
    x_send,
    x_recv,
    vec_rows,
    vec_send,
    vec_recv,
    qkv_full,
    dense_full,
    up_full,
    down_full,
    stat_send,
    stat_recv,
    part_qkv,
    sum_qkv,
    own_qkv,
    all_qkv,
    q_all,
    bias,
    score,
    weight,
    o_send,
    ml_send,
    o_recv,
    ml_recv,
    oz_recv,
    mlz_recv,
    dense_recv,
    att_send,
    att_recv,
    stat2_send,
    stat2_recv,
    part_up,
    sum_up,
    own_act,
    all_act,
    down_recv,
    mix_send,
    mix_recv,
    send_sem,
    recv_sem,
):
    rows = ROWS * GROUP
    requests = lengths.shape[1]
    slot_count = keys.shape[0]
    s = lax.axis_index("seq")
    y = lax.axis_index("mlp")
    z, a = s // GROUP, lax.rem(s, GROUP)

    def in_a(k):
        peer = lax.rem(a + k, GROUP)
        return peer, (z * GROUP + peer, y)

    def in_z(k):
        peer = lax.rem(z + k, GROUP)
        return peer, (peer * GROUP + a, y)

    def in_y(k):
        peer = lax.rem(y + k, GROUP)
        return peer, (s, peer)

    barrier = pltpu.get_barrier_semaphore()
    for ring in (in_a, in_z, in_y):
        for k in range(1, GROUP):
            pl.semaphore_signal(barrier, inc=1, device_id=ring(k)[1], device_id_type=MESH)

    started = []

    def exchange(stage, ring, source, target, me):
        copies = []
        for k in range(1, GROUP):
            peer, device = ring(k)
            copy = pltpu.make_async_remote_copy(
                src_ref=source(peer),
                dst_ref=target(me),
                send_sem=send_sem.at[stage, k],
                recv_sem=recv_sem.at[stage, k],
                device_id=device,
                device_id_type=MESH,
            )
            copy.start()
            copies.append(copy)
        started.extend(copies)

        def arrived():
            for copy in copies:
                copy.wait_recv()

        return arrived

    quarter = lax.rem(a, 4)
    spread = (iota((32, LANES), 1) == iota((32, LANES), 0) + 32 * quarter).astype(BF16)
    mine = jnp.zeros((rows, 32), F32)
    for t in range(STEPS):
        pick = (iota((rows, requests), 0) == STEPS * iota((rows, requests), 1) + t).astype(BF16)
        mine += dot_nt(pick, tokens[t])
    placed = dot(mine.astype(BF16), spread).astype(BF16).astype(F32)
    for b in range(GROUP):
        x_send[b] = placed[ROWS * b : ROWS * (b + 1)].astype(BF16)
    x_recv[a] = x_send[a]

    vec_rows[...] = jnp.zeros_like(vec_rows)
    for i, ref in enumerate((ln1_gain, ln1_bias, ln2_gain, ln2_bias, b_dense, b_down)):
        vec_rows[i : i + 1, :] = ref[...]
    vec_send[...] = jnp.dot(
        vec_rows[...],
        (iota((32, LANES), 1) == iota((32, LANES), 0) + 32 * quarter).astype(F32),
        preferred_element_type=F32,
        precision=lax.Precision.HIGHEST,
    )
    vec_recv[a] = vec_send[...]

    def block_of(ref):
        def at(i):
            return ref.at[pl.ds(pl.multiple_of(i * 32, 32), 32), :]

        return at

    qkv_full[pl.ds(pl.multiple_of(a * 32, 32), 32), :] = w_qkv[...]
    dense_full[pl.ds(pl.multiple_of(a * 32, 32), 32), :] = w_dense[...]
    up_full[pl.ds(pl.multiple_of(a * 32, 32), 32), :] = w_up[...]
    down_full[pl.ds(pl.multiple_of(a * 32, 32), 32), :] = w_down[...]

    pl.semaphore_wait(barrier, 3 * (GROUP - 1))

    x_here = exchange(0, in_a, lambda p: x_send.at[p], lambda m: x_recv.at[m], a)
    vec_here = exchange(1, in_a, lambda p: vec_send, lambda m: vec_recv.at[m], a)
    qkv_here = exchange(2, in_a, lambda p: w_qkv, block_of(qkv_full), a)
    dense_here = exchange(3, in_a, lambda p: w_dense, block_of(dense_full), a)
    up_here = exchange(4, in_a, lambda p: w_up, block_of(up_full), a)
    down_here = exchange(5, in_a, lambda p: w_down, block_of(down_full), a)

    def halves(slots):
        low = slots[0].astype(F32)
        high = slots[4].astype(F32)
        for i in range(1, 4):
            low = low + slots[i].astype(F32)
            high = high + slots[4 + i].astype(F32)
        return jnp.concatenate([low, high], axis=1)

    def statistics(tile):
        return to_row(
            [jnp.sum(tile, axis=1, keepdims=True), jnp.sum(tile * tile, axis=1, keepdims=True)]
        )

    def add_slots(slots):
        total = slots[0]
        for i in range(1, GROUP):
            total = total + slots[i]
        return total

    def normalize(tile, stats, gain, shift):
        mean = to_column(stats, 0) / features
        spread = to_column(stats, 1) / features - mean * mean
        return ((tile - mean) * lax.rsqrt(spread + EPS) * gain + shift).astype(BF16)

    x_here()
    x = halves(x_recv)
    stat_send[...] = statistics(x)
    stat_recv[z] = stat_send[...]
    stat_here = exchange(6, in_z, lambda p: stat_send, lambda m: stat_recv.at[m], z)

    half = 32
    position = (s * slot_count + iota((1, slot_count), 1)).astype(F32)
    for c in range(rows // half):
        row = iota((half, 1), 0) + half * c
        request, step = row >> 2, (row & 3).astype(F32)
        lane = iota((half, requests), 1)
        cached = jnp.broadcast_to(lengths[...], (half, requests)).astype(F32)
        start = jnp.sum(jnp.where(lane < request, cached + STEPS, 0.0), axis=1, keepdims=True)
        length = jnp.sum(jnp.where(lane == request, cached, 0.0), axis=1, keepdims=True)
        offset = position - start
        valid = (offset >= 0.0) & (offset < length)
        distance = (length + step) - offset
        for h in range(2):
            bias[h, half * c : half * (c + 1), :] = jnp.where(valid, -slopes[h] * distance, NEG)

    vec_here()
    vectors = halves(vec_recv)
    stat_here()
    normed = normalize(x, add_slots(stat_recv), vectors[0:1], vectors[1:2])

    qkv_here()
    partial = dot(normed, qkv_full[...])
    for j in range(6):
        part_qkv[j] = partial[:, LANES * j : LANES * (j + 1)]
    for j in range(6, GROUP):
        part_qkv[j] = jnp.zeros((ROWS, LANES), F32)
    sum_qkv[z] = part_qkv[z]
    exchange(7, in_z, lambda p: part_qkv.at[p], lambda m: sum_qkv.at[m], z)()
    own_qkv[...] = (add_slots(sum_qkv) + b_qkv[pl.ds(z, 1), :]).astype(BF16)
    all_qkv[z] = own_qkv[...]
    exchange(8, in_z, lambda p: own_qkv, lambda m: all_qkv.at[m], z)()
    for h in range(2):
        q_all[h, a] = all_qkv[3 * h]
    q0_here = exchange(9, in_a, lambda p: all_qkv.at[0], lambda m: q_all.at[0, m], a)
    q1_here = exchange(10, in_a, lambda p: all_qkv.at[3], lambda m: q_all.at[1, m], a)

    scale = 1.0 / math.sqrt(HD)
    fresh = []
    one, other = iota((ROWS, ROWS), 0), iota((ROWS, ROWS), 1)
    seen = ((one >> 2) == (other >> 2)) & ((other & 3) <= (one & 3))
    gap = ((one & 3) - (other & 3)).astype(F32)
    for h in range(2):
        near = dot_nt(all_qkv[3 * h], all_qkv[3 * h + 1]) * scale - slopes[h] * gap
        near = jnp.where(seen, near, NEG)
        top = jnp.max(near, axis=1, keepdims=True)
        share = jnp.exp(near - top)
        fresh.append(
            (dot(share.astype(BF16), all_qkv[3 * h + 2]), top, jnp.sum(share, axis=1, keepdims=True))
        )

    maxima, totals = [], []
    for h in range(2):
        (q0_here, q1_here)[h]()
        query = q_all[h].astype(F32).reshape(rows, HD).astype(BF16)
        score[...] = dot_nt(query, keys[:, HD * h : HD * (h + 1)])
        tops, sums = [], []
        for c in range(rows // half):
            span = slice(half * c, half * (c + 1))
            value = score[span, :] * scale + bias[h, span, :]
            top = jnp.maximum(jnp.max(value, axis=1, keepdims=True), FLOOR)
            share = jnp.exp(value - top)
            weight[span, :] = share.astype(BF16)
            tops.append(top)
            sums.append(jnp.sum(share, axis=1, keepdims=True))
        maxima.append(jnp.concatenate(tops, axis=0))
        totals.append(jnp.concatenate(sums, axis=0))
        out = dot(weight[...], values[:, HD * h : HD * (h + 1)])
        for b in range(GROUP):
            o_send[b, :, HD * h : HD * (h + 1)] = out[ROWS * b : ROWS * (b + 1)]
    for b in range(GROUP):
        span = slice(ROWS * b, ROWS * (b + 1))
        ml_send[b] = to_row([maxima[0][span], maxima[1][span], totals[0][span], totals[1][span]])
    o_recv[a] = o_send[a]
    ml_recv[a] = ml_send[a]
    ml_here = exchange(11, in_a, lambda p: ml_send.at[p], lambda m: ml_recv.at[m], a)
    o_here = exchange(12, in_a, lambda p: o_send.at[p], lambda m: o_recv.at[m], a)

    def combine(parts):
        top = parts[0][1]
        for part in parts[1:]:
            top = jnp.maximum(top, part[1])
        weighted, total = 0.0, 0.0
        for value, largest, amount in parts:
            factor = jnp.exp(largest - top)
            weighted = weighted + value * factor
            total = total + amount * factor
        return weighted, top, total

    def slots_of(o_ref, ml_ref, h):
        return [
            (
                o_ref[i, :, HD * h : HD * (h + 1)],
                to_column(ml_ref[i], h),
                to_column(ml_ref[i], 2 + h),
            )
            for i in range(GROUP)
        ]

    ml_here()
    o_here()
    merged = [combine(slots_of(o_recv, ml_recv, h)) for h in range(2)]
    for h in range(2):
        oz_recv[z, :, HD * h : HD * (h + 1)] = merged[h][0]
    mlz_recv[z] = to_row([merged[0][1], merged[1][1], merged[0][2], merged[1][2]])
    ml_here = exchange(13, in_z, lambda p: mlz_recv.at[z], lambda m: mlz_recv.at[m], z)
    o_here = exchange(14, in_z, lambda p: oz_recv.at[z], lambda m: oz_recv.at[m], z)
    ml_here()
    o_here()
    attention = []
    for h in range(2):
        weighted, _, total = combine(slots_of(oz_recv, mlz_recv, h) + [fresh[h]])
        attention.append((weighted / total).astype(BF16))
    attention = jnp.concatenate(attention, axis=1)

    dense_here()
    dense_recv[y] = dot_nt(attention, dense_full[...])
    exchange(15, in_y, lambda p: dense_recv.at[y], lambda m: dense_recv.at[m], y)()
    dense = add_slots(dense_recv) + vectors[4:5]
    hidden = (x + dense).astype(BF16).astype(F32)
    stat2_send[...] = statistics(hidden)
    stat2_recv[z] = stat2_send[...]
    stat2_here = exchange(16, in_z, lambda p: stat2_send, lambda m: stat2_recv.at[m], z)
    for i in range(2):
        att_send[i] = dense[:, LANES * i : LANES * (i + 1)].astype(BF16)
    att_recv[a] = att_send[a // 4]
    att_here = exchange(17, in_a, lambda p: att_send.at[p // 4], lambda m: att_recv.at[m], a)
    stat2_here()
    normed = normalize(hidden, add_slots(stat2_recv), vectors[2:3], vectors[3:4])

    up_here()
    partial = dot(normed, up_full[...])
    for j in range(GROUP):
        part_up[j] = partial[:, LANES * j : LANES * (j + 1)]
    sum_up[z] = part_up[z]
    exchange(18, in_z, lambda p: part_up.at[p], lambda m: sum_up.at[m], z)()
    own_act[...] = gelu_tanh(add_slots(sum_up) + b_up[pl.ds(z, 1), :]).astype(BF16)
    all_act[z] = own_act[...]
    act_here = exchange(19, in_z, lambda p: own_act, lambda m: all_act.at[m], z)

    def deliver(slots, out_ref):
        held = jnp.concatenate([slots[i].astype(F32) for i in range(GROUP)], axis=0)
        own = dot_nt(spread, held.astype(BF16)).astype(BF16)
        for t in range(STEPS):
            put = iota((rows, requests), 0) == STEPS * iota((rows, requests), 1) + t
            out_ref[t] = dot(own, put.astype(BF16)).astype(BF16)

    att_here()
    deliver(att_recv, attended_out)

    down_here()
    act_here()
    act = jnp.concatenate([all_act[i] for i in range(GROUP)], axis=1)
    down_recv[y] = dot_nt(act, down_full[...])
    exchange(20, in_y, lambda p: down_recv.at[y], lambda m: down_recv.at[m], y)()
    mixed = hidden + (add_slots(down_recv) + vectors[5:6])
    for i in range(2):
        mix_send[i] = mixed[:, LANES * i : LANES * (i + 1)].astype(BF16)
    mix_recv[a] = mix_send[a // 4]
    exchange(21, in_a, lambda p: mix_send.at[p // 4], lambda m: mix_recv.at[m], a)()
    deliver(mix_recv, mixed_out)

    for copy in started:
        copy.wait_send()


STAGES = 22


def local(
    tokens,
    lengths,
    slopes,
    ln1_gain,
    ln1_bias,
    w_qkv,
    b_qkv,
    keys,
    values,
    w_dense,
    b_dense,
    ln2_gain,
    ln2_bias,
    w_up,
    b_up,
    w_down,
    b_down,
):
    count, requests, width = tokens.shape
    features = width * lax.axis_size("seq")
    slot_count = keys.shape[0]
    rows = count * requests

    def as_row(vector):
        return vector.reshape(1, -1)

    bias_blocks = jnp.pad(b_qkv.reshape(6, LANES), ((0, 2), (0, 0)))
    vmem = pl.BlockSpec(memory_space=pltpu.VMEM)
    smem = pl.BlockSpec(memory_space=pltpu.SMEM)
    tile = (GROUP, ROWS, LANES)
    scratch = [
        pltpu.VMEM(tile, BF16),
        pltpu.VMEM(tile, BF16),
        pltpu.VMEM((8, 32), F32),
        pltpu.VMEM((8, LANES), F32),
        pltpu.VMEM((GROUP, 8, LANES), F32),
        pltpu.VMEM((256, 768), BF16),
        pltpu.VMEM((256, 256), BF16),
        pltpu.VMEM((256, 1024), BF16),
        pltpu.VMEM((256, 1024), BF16),
        pltpu.VMEM((1, LANES), F32),
        pltpu.VMEM((GROUP, 1, LANES), F32),
        pltpu.VMEM(tile, F32),
        pltpu.VMEM(tile, F32),
        pltpu.VMEM((ROWS, LANES), BF16),
        pltpu.VMEM(tile, BF16),
        pltpu.VMEM((2, GROUP, ROWS, LANES), BF16),
        pltpu.VMEM((2, rows, slot_count), F32),
        pltpu.VMEM((rows, slot_count), F32),
        pltpu.VMEM((rows, slot_count), BF16),
        pltpu.VMEM((GROUP, ROWS, 256), F32),
        pltpu.VMEM((GROUP, 1, LANES), F32),
        pltpu.VMEM((GROUP, ROWS, 256), F32),
        pltpu.VMEM((GROUP, 1, LANES), F32),
        pltpu.VMEM((GROUP, ROWS, 256), F32),
        pltpu.VMEM((GROUP, 1, LANES), F32),
        pltpu.VMEM((GROUP, ROWS, 256), F32),
        pltpu.VMEM((2, ROWS, LANES), BF16),
        pltpu.VMEM(tile, BF16),
        pltpu.VMEM((1, LANES), F32),
        pltpu.VMEM((GROUP, 1, LANES), F32),
        pltpu.VMEM(tile, F32),
        pltpu.VMEM(tile, F32),
        pltpu.VMEM((ROWS, LANES), BF16),
        pltpu.VMEM(tile, BF16),
        pltpu.VMEM((GROUP, ROWS, 256), F32),
        pltpu.VMEM((2, ROWS, LANES), BF16),
        pltpu.VMEM(tile, BF16),
        pltpu.SemaphoreType.DMA((STAGES, GROUP)),
        pltpu.SemaphoreType.DMA((STAGES, GROUP)),
    ]
    shape = jax.ShapeDtypeStruct((count, width, requests), BF16)

    def body(*refs):
        kernel(features, *refs)

    attended, mixed = pl.pallas_call(
        body,
        out_shape=(shape, shape),
        in_specs=[vmem, vmem, smem] + [vmem] * 14,
        out_specs=(vmem, vmem),
        scratch_shapes=scratch,
        compiler_params=pltpu.CompilerParams(collective_id=0, has_side_effects=True),
        name="layer",
    )(
        tokens.transpose(0, 2, 1),
        as_row(lengths),
        slopes,
        as_row(ln1_gain),
        as_row(ln1_bias),
        w_qkv,
        bias_blocks,
        keys,
        values,
        w_dense.T,
        as_row(b_dense),
        as_row(ln2_gain),
        as_row(ln2_bias),
        w_up,
        b_up.reshape(GROUP, LANES),
        w_down.T,
        as_row(b_down),
    )
    return attended.transpose(0, 2, 1), mixed.transpose(0, 2, 1)


def solution(mesh):
    in_specs = (
        P(None, None, "seq"),
        P(),
        P("mlp"),
        P("seq"),
        P("seq"),
        P("seq", "mlp"),
        P("mlp"),
        P("seq", "mlp"),
        P("seq", "mlp"),
        P("mlp", "seq"),
        P("seq"),
        P("seq"),
        P("seq"),
        P("seq", "mlp"),
        P("mlp"),
        P("mlp", "seq"),
        P("seq"),
    )
    out_specs = (P(None, None, "seq"), P(None, None, "seq"))
    return jax.shard_map(local, mesh=mesh, in_specs=in_specs, out_specs=out_specs, check_vma=False)
```

time: 1070 us -> 95.6 us (0.09)
  blocking collectives: 562 us -> 0 us
  waiting for transfers between devices: 438 us -> 0 us
  Pallas kernels: 0 us -> 91.5 us
  local copies, waits for them, and re-layouts: 30 us -> 3.27 us
  between operations: 14.1 us -> 0.66 us
  matrix products: 11.2 us -> 0 us
    psum x3 -> x0, waiting for transfers between devices: 438 us -> none  [the longest x1 190 us: local(): rounded = (lax.psum(partial_qkv, 'seq') + b_qkv).astype(jnp.bfloat16)]
    psum x5 -> x0, blocking collectives: 437 us -> none  [the longest x1 133 us: local(): lax.psum((jnp.sum(hidden_full, axis=-1), jnp.sum(hidden_full * hidden_ful...]
    pmax x1 -> x0, blocking collectives: 126 us -> none  [local(): top = lax.pmax(maxima, 'seq')]
    pallas_call x0 -> x1, Pallas kernels: none -> 91.5 us  [local(): pl.pallas_call(body, out_shape=(shape, shape), in_specs=[vmem, vmem, smem...]
    dot_general x28 -> x0, matrix products: 11.2 us -> none  [the longest x8 2.88 us: visit(): jnp.einsum('jr,jc->rc', member_full, product, precision=lax.Precision.HIG...]
  transfers between devices with their start and end apart: 3 -> 0, of which waited for: 3 -> 0; matrix products, arithmetic and copies ran while one was open for 0% -> 0% of each run, Pallas kernels for 0% -> 0%
where the time goes in v1:
time: 95.6 us; the launch traced here: 95.4 us
  Pallas kernels  91.5 us (96%)
  local copies, waits for them, and re-layouts  3.27 us (3%)
    pallas_call x1, Pallas kernels, local(): pl.pallas_call(body, out_shape=(shape, shape), in_specs=[vmem, vmem, smem...  91.5 us
    unnamed x6, local copies, waits for them, and re-layouts  2.68 us

profile of v1, /device:TPU:1, one launch (start us, length us, event | category | flops | bytes accessed | tf_op | source)
XLA Modules:
  0.0 95.4 jit_solution(1987397096225401890)
XLA Ops:
  0.6 0.0 copy-start.1
  0.6 0.7 copy-done.1
  1.3 0.6 pad.4.refs_6_
  1.9 91.5 %layer.1 = (bf16[4,32,48]{2,1,0:T(8,128)(2,1)}, bf16[4,32,48]{2,1,0:T(8,128)(2,1)}) custom-call(bf16[4,32,48]{2,1,0:T(8,128)(2,1)} %bitcast.15, s32[1,48]{1,0:T(1,128)} %bitcast.21, f32[2]{0:T(128)} %refs_2_.1, f32[1,32]{1,0:T(1,128)} %bitcast.22, f32[1,32]{1,0:T(1,128)} %bitcast.23, bf16[32,768]{1,0:T(8,128)(2,1)} %refs_5_.1, f32[8,128]{1,0:T(8,128)} %pad.4.refs_6_, ...), custom_call_target="tpu_custom_call" | custom-call | tf_op jit(solution)/shard_map/layer/pallas_call | solution.py:484
  93.4 0.0 copy-start
  93.4 1.4 %copy.21 = bf16[4,48,32]{1,2,0:T(8,128)(2,1)} copy(bf16[4,48,32]{1,2,0:T(8,128)(2,1)} %bitcast.17) | data formatting | bytes 24576
  94.8 0.0 copy-done
  94.8 0.6 copy.22
Async XLA Ops:
  0.6 0.7 copy-start.1
  93.4 1.4 %copy-start = (bf16[4,32,48]{2,1,0:T(8,128)(2,1)S(1)}, bf16[4,32,48]{2,1,0:T(8,128)(2,1)}, u32[]{:S(2)}) copy-start(bf16[4,32,48]{2,1,0:T(8,128)(2,1)} %get-tuple-element.5) | copy-start | bytes 36868

commit v2 on v1

--- a/solution.py
+++ b/solution.py
@@ -64,8 +64,8 @@
     ln1_bias,
     w_qkv,
     b_qkv,
-    keys,
-    values,
+    keys_far,
+    values_far,
     w_dense,
     b_dense,
     ln2_gain,
@@ -104,8 +104,6 @@
     dense_recv,
     att_send,
     att_recv,
-    stat2_send,
-    stat2_recv,
     part_up,
     sum_up,
     own_act,
@@ -113,8 +111,11 @@
     down_recv,
     mix_send,
     mix_recv,
+    keys,
+    values,
     send_sem,
     recv_sem,
+    load_sem,
 ):
     rows = ROWS * GROUP
     requests = lengths.shape[1]
@@ -164,6 +165,21 @@
 
         return arrived
 
+    own = pl.ds(pl.multiple_of(a * 32, 32), 32)
+    loads = []
+    for i, (source, target) in enumerate(
+        (
+            (w_dense, dense_full.at[own, :]),
+            (w_up, up_full.at[own, :]),
+            (w_down, down_full.at[own, :]),
+            (keys_far, keys),
+            (values_far, values),
+        )
+    ):
+        load = pltpu.make_async_copy(source, target, load_sem.at[i])
+        load.start()
+        loads.append(load)
+
     quarter = lax.rem(a, 4)
     spread = (iota((32, LANES), 1) == iota((32, LANES), 0) + 32 * quarter).astype(BF16)
     mine = jnp.zeros((rows, 32), F32)
@@ -192,19 +208,19 @@
 
         return at
 
-    qkv_full[pl.ds(pl.multiple_of(a * 32, 32), 32), :] = w_qkv[...]
-    dense_full[pl.ds(pl.multiple_of(a * 32, 32), 32), :] = w_dense[...]
-    up_full[pl.ds(pl.multiple_of(a * 32, 32), 32), :] = w_up[...]
-    down_full[pl.ds(pl.multiple_of(a * 32, 32), 32), :] = w_down[...]
+    qkv_full[own, :] = w_qkv[...]
 
     pl.semaphore_wait(barrier, 3 * (GROUP - 1))
 
     x_here = exchange(0, in_a, lambda p: x_send.at[p], lambda m: x_recv.at[m], a)
     vec_here = exchange(1, in_a, lambda p: vec_send, lambda m: vec_recv.at[m], a)
     qkv_here = exchange(2, in_a, lambda p: w_qkv, block_of(qkv_full), a)
-    dense_here = exchange(3, in_a, lambda p: w_dense, block_of(dense_full), a)
-    up_here = exchange(4, in_a, lambda p: w_up, block_of(up_full), a)
-    down_here = exchange(5, in_a, lambda p: w_down, block_of(down_full), a)
+    loads[0].wait()
+    dense_here = exchange(3, in_a, lambda p: dense_full.at[own, :], block_of(dense_full), a)
+    loads[1].wait()
+    up_here = exchange(4, in_a, lambda p: up_full.at[own, :], block_of(up_full), a)
+    loads[2].wait()
+    down_here = exchange(5, in_a, lambda p: down_full.at[own, :], block_of(down_full), a)
 
     def halves(slots):
         low = slots[0].astype(F32)
@@ -220,21 +236,15 @@
         )
 
     def add_slots(slots):
-        total = slots[0]
+        total = slots[0].astype(F32)
         for i in range(1, GROUP):
-            total = total + slots[i]
+            total = total + slots[i].astype(F32)
         return total
 
     def normalize(tile, stats, gain, shift):
         mean = to_column(stats, 0) / features
         spread = to_column(stats, 1) / features - mean * mean
         return ((tile - mean) * lax.rsqrt(spread + EPS) * gain + shift).astype(BF16)
-
-    x_here()
-    x = halves(x_recv)
-    stat_send[...] = statistics(x)
-    stat_recv[z] = stat_send[...]
-    stat_here = exchange(6, in_z, lambda p: stat_send, lambda m: stat_recv.at[m], z)
 
     half = 32
     position = (s * slot_count + iota((1, slot_count), 1)).astype(F32)
@@ -251,6 +261,12 @@
         for h in range(2):
             bias[h, half * c : half * (c + 1), :] = jnp.where(valid, -slopes[h] * distance, NEG)
 
+    x_here()
+    x = halves(x_recv)
+    stat_send[...] = statistics(x)
+    stat_recv[z] = stat_send[...]
+    stat_here = exchange(6, in_z, lambda p: stat_send, lambda m: stat_recv.at[m], z)
+
     vec_here()
     vectors = halves(vec_recv)
     stat_here()
@@ -264,7 +280,7 @@
         part_qkv[j] = jnp.zeros((ROWS, LANES), F32)
     sum_qkv[z] = part_qkv[z]
     exchange(7, in_z, lambda p: part_qkv.at[p], lambda m: sum_qkv.at[m], z)()
-    own_qkv[...] = (add_slots(sum_qkv) + b_qkv[pl.ds(z, 1), :]).astype(BF16)
+    own_qkv[...] = (add_slots(sum_qkv) + b_qkv[pl.ds(jnp.minimum(z, 5), 1), :]).astype(BF16)
     all_qkv[z] = own_qkv[...]
     exchange(8, in_z, lambda p: own_qkv, lambda m: all_qkv.at[m], z)()
     for h in range(2):
@@ -286,6 +302,8 @@
             (dot(share.astype(BF16), all_qkv[3 * h + 2]), top, jnp.sum(share, axis=1, keepdims=True))
         )
 
+    loads[3].wait()
+    loads[4].wait()
     maxima, totals = [], []
     for h in range(2):
         (q0_here, q1_here)[h]()
@@ -304,7 +322,7 @@
         totals.append(jnp.concatenate(sums, axis=0))
         out = dot(weight[...], values[:, HD * h : HD * (h + 1)])
         for b in range(GROUP):
-            o_send[b, :, HD * h : HD * (h + 1)] = out[ROWS * b : ROWS * (b + 1)]
+            o_send[b, :, HD * h : HD * (h + 1)] = out[ROWS * b : ROWS * (b + 1)].astype(BF16)
     for b in range(GROUP):
         span = slice(ROWS * b, ROWS * (b + 1))
         ml_send[b] = to_row([maxima[0][span], maxima[1][span], totals[0][span], totals[1][span]])
@@ -327,7 +345,7 @@
     def slots_of(o_ref, ml_ref, h):
         return [
             (
-                o_ref[i, :, HD * h : HD * (h + 1)],
+                o_ref[i, :, HD * h : HD * (h + 1)].astype(F32),
                 to_column(ml_ref[i], h),
                 to_column(ml_ref[i], 2 + h),
             )
@@ -338,7 +356,7 @@
     o_here()
     merged = [combine(slots_of(o_recv, ml_recv, h)) for h in range(2)]
     for h in range(2):
-        oz_recv[z, :, HD * h : HD * (h + 1)] = merged[h][0]
+        oz_recv[z, :, HD * h : HD * (h + 1)] = merged[h][0].astype(BF16)
     mlz_recv[z] = to_row([merged[0][1], merged[1][1], merged[0][2], merged[1][2]])
     ml_here = exchange(13, in_z, lambda p: mlz_recv.at[z], lambda m: mlz_recv.at[m], z)
     o_here = exchange(14, in_z, lambda p: oz_recv.at[z], lambda m: oz_recv.at[m], z)
@@ -351,27 +369,36 @@
     attention = jnp.concatenate(attention, axis=1)
 
     dense_here()
-    dense_recv[y] = dot_nt(attention, dense_full[...])
+    dense_recv[y] = dot_nt(attention, dense_full[...]).astype(BF16)
     exchange(15, in_y, lambda p: dense_recv.at[y], lambda m: dense_recv.at[m], y)()
     dense = add_slots(dense_recv) + vectors[4:5]
     hidden = (x + dense).astype(BF16).astype(F32)
-    stat2_send[...] = statistics(hidden)
-    stat2_recv[z] = stat2_send[...]
-    stat2_here = exchange(16, in_z, lambda p: stat2_send, lambda m: stat2_recv.at[m], z)
+
+    up_here()
+    gain, shift = vectors[2:3], vectors[3:4]
+    left = jnp.concatenate([hidden * gain, gain, shift, jnp.zeros((6, gain.shape[1]), F32)], axis=0)
+    coarse = left.astype(BF16)
+    fine = (left - coarse.astype(F32)).astype(BF16)
+    partial = dot(coarse, up_full[...]) + dot(fine, up_full[...])
+    last = iota((8, LANES), 0)
+    sums = statistics(hidden)
+    for j in range(GROUP):
+        block = partial[:, LANES * j : LANES * (j + 1)]
+        part_up[j, 0:ROWS] = block[:ROWS]
+        part_up[j, ROWS : ROWS + 8] = jnp.where(last == 2, sums, block[ROWS:])
+    sum_up[z] = part_up[z]
+    sum_here = exchange(18, in_z, lambda p: part_up.at[p], lambda m: sum_up.at[m], z)
     for i in range(2):
         att_send[i] = dense[:, LANES * i : LANES * (i + 1)].astype(BF16)
     att_recv[a] = att_send[a // 4]
     att_here = exchange(17, in_a, lambda p: att_send.at[p // 4], lambda m: att_recv.at[m], a)
-    stat2_here()
-    normed = normalize(hidden, add_slots(stat2_recv), vectors[2:3], vectors[3:4])
-
-    up_here()
-    partial = dot(normed, up_full[...])
-    for j in range(GROUP):
-        part_up[j] = partial[:, LANES * j : LANES * (j + 1)]
-    sum_up[z] = part_up[z]
-    exchange(18, in_z, lambda p: part_up.at[p], lambda m: sum_up.at[m], z)()
-    own_act[...] = gelu_tanh(add_slots(sum_up) + b_up[pl.ds(z, 1), :]).astype(BF16)
+    sum_here()
+    total = add_slots(sum_up)
+    gained, shifted, stats = (total[ROWS + i : ROWS + i + 1] for i in range(3))
+    mean = to_column(stats, 0) / features
+    variance = to_column(stats, 1) / features - mean * mean
+    upward = lax.rsqrt(variance + EPS) * (total[:ROWS] - mean * gained) + shifted
+    own_act[...] = gelu_tanh(upward + b_up[pl.ds(z, 1), :]).astype(BF16)
     all_act[z] = own_act[...]
     act_here = exchange(19, in_z, lambda p: own_act, lambda m: all_act.at[m], z)
 
@@ -388,7 +415,7 @@
     down_here()
     act_here()
     act = jnp.concatenate([all_act[i] for i in range(GROUP)], axis=1)
-    down_recv[y] = dot_nt(act, down_full[...])
+    down_recv[y] = dot_nt(act, down_full[...]).astype(BF16)
     exchange(20, in_y, lambda p: down_recv.at[y], lambda m: down_recv.at[m], y)()
     mixed = hidden + (add_slots(down_recv) + vectors[5:6])
     for i in range(2):
@@ -431,9 +458,9 @@
     def as_row(vector):
         return vector.reshape(1, -1)
 
-    bias_blocks = jnp.pad(b_qkv.reshape(6, LANES), ((0, 2), (0, 0)))
     vmem = pl.BlockSpec(memory_space=pltpu.VMEM)
     smem = pl.BlockSpec(memory_space=pltpu.SMEM)
+    far = pl.BlockSpec(memory_space=pl.ANY)
     tile = (GROUP, ROWS, LANES)
     scratch = [
         pltpu.VMEM(tile, BF16),
@@ -455,26 +482,27 @@
         pltpu.VMEM((2, rows, slot_count), F32),
         pltpu.VMEM((rows, slot_count), F32),
         pltpu.VMEM((rows, slot_count), BF16),
-        pltpu.VMEM((GROUP, ROWS, 256), F32),
+        pltpu.VMEM((GROUP, ROWS, 256), BF16),
         pltpu.VMEM((GROUP, 1, LANES), F32),
-        pltpu.VMEM((GROUP, ROWS, 256), F32),
+        pltpu.VMEM((GROUP, ROWS, 256), BF16),
         pltpu.VMEM((GROUP, 1, LANES), F32),
-        pltpu.VMEM((GROUP, ROWS, 256), F32),
+        pltpu.VMEM((GROUP, ROWS, 256), BF16),
         pltpu.VMEM((GROUP, 1, LANES), F32),
-        pltpu.VMEM((GROUP, ROWS, 256), F32),
+        pltpu.VMEM((GROUP, ROWS, 256), BF16),
         pltpu.VMEM((2, ROWS, LANES), BF16),
         pltpu.VMEM(tile, BF16),
-        pltpu.VMEM((1, LANES), F32),
-        pltpu.VMEM((GROUP, 1, LANES), F32),
-        pltpu.VMEM(tile, F32),
-        pltpu.VMEM(tile, F32),
+        pltpu.VMEM((GROUP, ROWS + 8, LANES), F32),
+        pltpu.VMEM((GROUP, ROWS + 8, LANES), F32),
         pltpu.VMEM((ROWS, LANES), BF16),
         pltpu.VMEM(tile, BF16),
-        pltpu.VMEM((GROUP, ROWS, 256), F32),
+        pltpu.VMEM((GROUP, ROWS, 256), BF16),
         pltpu.VMEM((2, ROWS, LANES), BF16),
         pltpu.VMEM(tile, BF16),
+        pltpu.VMEM((slot_count, 256), BF16),
+        pltpu.VMEM((slot_count, 256), BF16),
         pltpu.SemaphoreType.DMA((STAGES, GROUP)),
         pltpu.SemaphoreType.DMA((STAGES, GROUP)),
+        pltpu.SemaphoreType.DMA((5,)),
     ]
     shape = jax.ShapeDtypeStruct((count, width, requests), BF16)
 
@@ -484,7 +512,7 @@
     attended, mixed = pl.pallas_call(
         body,
         out_shape=(shape, shape),
-        in_specs=[vmem, vmem, smem] + [vmem] * 14,
+        in_specs=[vmem, vmem, smem] + [vmem] * 4 + [far] * 3 + [vmem] * 3 + [far] + [vmem] + [far] + [vmem],
         out_specs=(vmem, vmem),
         scratch_shapes=scratch,
         compiler_params=pltpu.CompilerParams(collective_id=0, has_side_effects=True),
@@ -496,7 +524,7 @@
         as_row(ln1_gain),
         as_row(ln1_bias),
         w_qkv,
-        bias_blocks,
+        b_qkv.reshape(6, LANES),
         keys,
         values,
         w_dense.T,

time: 95.6 us -> 82.7 us (0.87)
  Pallas kernels: 91.5 us -> 79.8 us
  local copies, waits for them, and re-layouts: 3.27 us -> 2 us
    pallas_call x1, Pallas kernels: 91.5 us -> 79.8 us  [local(): pl.pallas_call(body, out_shape=(shape, shape), in_specs=[vmem, vmem, smem...]
    unnamed x6 -> x4, local copies, waits for them, and re-layouts: 2.68 us -> 2 us
where the time goes in v2:
time: 82.7 us; the launch traced here: 82.4 us
  Pallas kernels  79.8 us (96%)
  local copies, waits for them, and re-layouts  2 us (2%)
    pallas_call x1, Pallas kernels, local(): pl.pallas_call(body, out_shape=(shape, shape), in_specs=[vmem, vmem, smem...  79.8 us
    unnamed x4, local copies, waits for them, and re-layouts  2 us

profile of v2, /device:TPU:1, one launch (start us, length us, event | category | flops | bytes accessed | tf_op | source)
XLA Modules:
  0.0 82.4 jit_solution(3734102433173422173)
XLA Ops:
  0.6 79.8 %layer.1 = (bf16[4,32,48]{2,1,0:T(8,128)(2,1)}, bf16[4,32,48]{2,1,0:T(8,128)(2,1)}) custom-call(bf16[4,32,48]{2,1,0:T(8,128)(2,1)} %bitcast.15, s32[1,48]{1,0:T(1,128)} %bitcast.21, f32[2]{0:T(128)} %refs_2_.1, f32[1,32]{1,0:T(1,128)} %bitcast.22, f32[1,32]{1,0:T(1,128)} %bitcast.23, bf16[32,768]{1,0:T(8,128)(2,1)} %refs_5_.1, f32[6,128]{1,0:T(8,128)} %bitcast.19, ...), custom_call_target="tpu_custom_call" | custom-call | tf_op jit(solution)/shard_map/layer/pallas_call | solution.py:512
  80.4 0.0 copy-start
  80.4 1.4 %copy.21 = bf16[4,48,32]{1,2,0:T(8,128)(2,1)} copy(bf16[4,48,32]{1,2,0:T(8,128)(2,1)} %bitcast.17) | data formatting | bytes 24576
  81.8 0.0 copy-done
  81.8 0.6 copy.22
Async XLA Ops:
  80.4 1.4 %copy-start = (bf16[4,32,48]{2,1,0:T(8,128)(2,1)S(1)}, bf16[4,32,48]{2,1,0:T(8,128)(2,1)}, u32[]{:S(2)}) copy-start(bf16[4,32,48]{2,1,0:T(8,128)(2,1)} %get-tuple-element.5) | copy-start | bytes 36868
